TPU v7x, 512 devices: a whole 4x4x16 slice. The times are simulated.
512 devices in a mesh: replica: 4 (over z_hi, core), inner: 128 (over z_lo, x, y).
Axes of the slice: x: 4, y: 4, z: 16 (z_hi: 2, z_lo: 8; z = z_hi * 8 + z_lo), core: 2. Of those that a mesh axis runs over, the one named last changes fastest.
Arguments:
- square_weights: float32 [2, 1024, 1024], P(None, 'inner'), may hold values from -6 to 6
- square_copies: float32 [4, 2, 1024, 1024], P('replica', None, 'inner'), may hold values from -6 to 6
- square_moment: float32 [2, 1024, 1024], P(None, 'inner'), may hold values from -6 to 6
- broad_weights: float32 [2, 1024, 2048], P(None, 'inner'), may hold values from -6 to 6
- broad_copies: float32 [4, 2, 1024, 2048], P('replica', None, 'inner'), may hold values from -6 to 6
- broad_moment: float32 [2, 1024, 2048], P(None, 'inner'), may hold values from -6 to 6
- embed_weights: float32 [16384, 1024], P('inner'), may hold values from -6 to 6
- embed_copies: float32 [4, 16384, 1024], P('replica', 'inner'), may hold values from -90 to 90, as said below
- embed_moment: float32 [16384, 1024], P('inner'), may hold values from -6 to 6
- embed_error: float32 [4, 16384, 1024], P('replica', 'inner'), may hold values from -3 to 3
- warm_start: float32 [64, 1024], replicated, may hold values from -6 to 6
Outputs:
- square_updated: float32 [2, 1024, 1024], P(None, 'inner')
- square_velocity: float32 [2, 1024, 1024], P(None, 'inner')
- broad_updated: float32 [2, 1024, 2048], P(None, 'inner')
- broad_velocity: float32 [2, 1024, 2048], P(None, 'inner')
- embed_updated: float32 [16384, 1024], P('inner')
- embed_velocity: float32 [16384, 1024], P('inner')
- embed_carried: float32 [4, 16384, 1024], P('replica', 'inner')
Inputs may be any that keep to these rules, and one draw needn't show every extreme that they name: `embed_copies`: each replica's embedding after its inner steps.
All inputs are finite; a program needn't handle non-finite values.
Results may differ from a plain program's by a relative error of at most 0.0001.
Values sent between devices are 32-bit elements; how exact they have to be, the bound alone decides.
A program may use at most 64 MiB of HBM per device.

v0:
```python
import jax
import jax.numpy as jnp
from jax import lax
from jax.sharding import PartitionSpec as P

outer_rate = 0.7
momentum_decay = 0.9


def nesterov(weights, gradient, moment):
    velocity = momentum_decay * moment + gradient
    return (weights - outer_rate * (gradient + momentum_decay * velocity), velocity)


def local(
    square_weights,
    square_copies,
    square_moment,
    broad_weights,
    broad_copies,
    broad_moment,
    embed_weights,
    embed_copies,
    embed_moment,
    embed_error,
    warm_start,
):
    replicas = lax.axis_size("replica")
    highest = lax.Precision.HIGHEST
    contract_last = (((1,), (1,)), ((), ()))
    square_term = square_weights - square_copies[0]
    broad_term = broad_weights - broad_copies[0]
    corrected = embed_weights - embed_copies[0] + embed_error[0]
    square_sum, broad_sum = lax.psum((square_term, broad_term), "replica")
    left_local = lax.dot_general(warm_start, corrected, contract_last, precision=highest)
    left_factor = lax.psum(left_local, "replica") / replicas
    gram_local = lax.dot_general(left_factor, left_factor, contract_last, precision=highest)
    gram_matrix = lax.psum(gram_local, "inner")
    lower_factor = jnp.linalg.cholesky(gram_matrix)
    basis_rows = lax.linalg.triangular_solve(lower_factor, left_factor, left_side=True, lower=True)
    right_term = jnp.dot(basis_rows, corrected, precision=highest)
    right_total = lax.psum(right_term, ("replica", "inner"))
    right_factor = right_total / replicas
    embed_step = lax.dot_general(
        basis_rows, right_factor, (((0,), (0,)), ((), ())), precision=highest
    )
    embed_updated, embed_velocity = nesterov(embed_weights, embed_step, embed_moment)
    square_updated, square_velocity = nesterov(square_weights, square_sum / replicas, square_moment)
    broad_updated, broad_velocity = nesterov(broad_weights, broad_sum / replicas, broad_moment)
    embed_carried = (corrected - embed_step)[None]
    return (
        square_updated,
        square_velocity,
        broad_updated,
        broad_velocity,
        embed_updated,
        embed_velocity,
        embed_carried,
    )


def solution(mesh):
    in_specs = (
        P(None, "inner", None),
        P("replica", None, "inner", None),
        P(None, "inner", None),
        P(None, "inner", None),
        P("replica", None, "inner", None),
        P(None, "inner", None),
        P("inner", None),
        P("replica", "inner", None),
        P("inner", None),
        P("replica", "inner", None),
        P(),
    )
    out_specs = (
        P(None, "inner", None),
        P(None, "inner", None),
        P(None, "inner", None),
        P(None, "inner", None),
        P("inner", None),
        P("inner", None),
        P("replica", "inner", None),
    )
    return jax.shard_map(local, mesh=mesh, in_specs=in_specs, out_specs=out_specs, check_vma=False)
```

profile of v0, /device:TPU:1, one launch (start us, length us, event | category | flops | bytes accessed | tf_op | source)
XLA Modules:
  0.0 1638.2 jit_solution(11594696563197630290)
XLA Ops:
  7.2 0.0 copy-start
  7.2 0.0 all-reduce.4.cloned.1.call-start
  7.2 1.5 bitcast_add_fusion
  8.7 0.0 copy-done
  8.7 0.7 convolution_bitcast_fusion
  9.4 33.8 %psum.37 = f32[64,128]{1,0:T(8,128)S(1)} all-reduce(f32[64,128]{1,0:T(8,128)S(1)} %convolution_bitcast_fusion), channel_id=1, replica_groups=mesh['replica'=4,'inner'=128] {'replica'}, use_global_device_ids=true, to_apply=%region_2.0 | all-reduce | flops 8192 | bytes 65536 | tf_op jit(solution)/shard_map/psum | solution.py:36
  43.2 0.2 fusion.8
  43.4 926.7 %psum.38 = f32[64,64]{0,1:T(8,128)S(1)} all-reduce(f32[64,64]{0,1:T(8,128)S(1)} %fusion.8), channel_id=1, replica_groups=mesh['replica'=4,'inner'=128] {'inner'}, use_global_device_ids=true, to_apply=%region_3.0 | all-reduce | flops 4096 | bytes 32768 | tf_op jit(solution)/shard_map/psum | solution.py:38
  970.1 0.1 copy.19
  970.2 5.8 cholesky.16
  976.1 0.6 compare_reduce_fusion
  976.7 0.7 fusion.3
  977.4 4.9 custom-call.6
  982.3 0.3 fusion.4
  982.5 0.0 copy-start.2
  982.5 0.0 copy-start.5
  982.6 0.0 copy-start.4
  982.6 0.0 copy-start.7
  982.6 1.1 fusion.17
  983.7 0.0 copy-start.1
  983.7 0.0 copy-start.3
  983.7 0.0 all-reduce.4.cloned.1.call-update
  983.8 0.0 all-reduce.6.cloned.1.call-start
  983.8 0.0 copy-done.2
  983.8 0.0 copy-done.5
  983.8 0.7 bitcast_subtract_fusion.1
  984.5 0.0 copy-done.4
  984.5 0.0 copy-done.7
  984.5 0.6 bitcast_subtract_fusion.2
  985.1 0.0 all-reduce.6.cloned.1.call-update
  985.2 0.0 copy-start.6
  985.2 561.2 %all-reduce.4.cloned.1.call-done = f32[64,1024]{1,0:T(8,128)} async-done(((f32[64,1024]{1,0:T(8,128)}), f32[64,1024]{1,0:T(8,128)}) %all-reduce.4.cloned.1.call-update) | async-done | bytes 262160 | tf_op jit(solution)/shard_map/psum | solution.py:42
  1546.4 0.0 copy-done.1
  1546.4 0.0 copy-done.3
  1546.4 2.8 multiply_subtract_fusion
  1549.2 79.8 %all-reduce.6.cloned.1.call-done = (f32[2,8,1024]{2,1,0:T(8,128)}, f32[2,8,2048]{2,1,0:T(8,128)}) async-done(((f32[2,8,1024]{2,1,0:T(8,128)}, f32[2,8,2048]{2,1,0:T(8,128)}), (f32[2,8,1024]{2,1,0:T(8,128)}, f32[2,8,2048]{2,1,0:T(8,128)})) %all-reduce.6.cloned.1.call-update) | async-done | bytes 196624 | tf_op jit(solution)/shard_map/psum | solution.py:34
  1629.1 0.0 copy-done.6
  1629.1 0.0 copy-start.8
  1629.1 0.0 copy-start.9
  1629.1 1.7 multiply_subtract_fusion.1
  1630.7 0.0 copy-done.8
  1630.7 0.0 copy-done.9
  1630.7 0.7 multiply_subtract_fusion.2
  (2 shorter events, 0.0 us)
Async XLA Ops:
  7.2 1.6 copy-start
  7.2 1539.2 %all-reduce.4.cloned.1.call-start = ((), (), s32[]{:S(2)}) async-start(), calls=%async_computation | async-start | bytes 524288 | tf_op jit(solution)/shard_map/psum | solution.py:42
  982.5 1.3 copy-start.2
  982.5 1.3 copy-start.5
  982.6 1.9 copy-start.4
  982.6 1.9 copy-start.7
  983.7 562.7 %copy-start.1 = (f32[128,1024]{1,0:T(8,128)S(1)}, f32[128,1024]{1,0:T(8,128)}, u32[]{:S(2)}) copy-start(f32[128,1024]{1,0:T(8,128)} %param.17) | copy-start | bytes 1572868
  983.7 562.7 %copy-start.3 = (f32[128,1024]{1,0:T(8,128)S(1)}, f32[128,1024]{1,0:T(8,128)}, u32[]{:S(2)}) copy-start(f32[128,1024]{1,0:T(8,128)} %param.19) | copy-start | bytes 1572868
  983.8 645.3 %all-reduce.6.cloned.1.call-start = ((), (), s32[]{:S(2)}) async-start(), calls=%async_computation.1 | async-start | bytes 393216 | tf_op jit(solution)/shard_map/psum | solution.py:34
  985.2 643.9 %copy-start.6 = (f32[2,8,2048]{2,1,0:T(8,128)S(1)}, f32[2,8,2048]{2,1,0:T(8,128)}, u32[]{:S(2)}) copy-start(f32[2,8,2048]{2,1,0:T(8,128)} %param.16) | copy-start | bytes 393220
  1629.1 1.7 copy-start.8
  1629.1 1.7 copy-start.9
Sparse Core Ops, SparseCore 0:
  983.9 562.4 all-reduce.3
  1550.2 78.7 all-reduce.5
where the time goes:
time: 1640 us
  blocking collectives  961 us (59%)
  waiting for transfers between devices  641 us (39%)
  other arithmetic  17.2 us (1%)
    psum x1, blocking collectives, local(): gram_matrix = lax.psum(gram_local, 'inner')  927 us
    psum x1, waiting for transfers between devices, local(): right_total = lax.psum(right_term, ('replica', 'inner'))  561 us
    psum x1, waiting for transfers between devices, local(): square_sum, broad_sum = lax.psum((square_term, broad_term), 'replica')  79.8 us
    psum x1, blocking collectives, local(): left_factor = lax.psum(left_local, 'replica') / replicas  33.8 us
  transfers between devices with their start and end apart: 2, of which 2 were waited for; matrix products, arithmetic and copies ran while one was open for 0% of the time, Pallas kernels for 0%

commit v1 on v0

--- a/solution.py
+++ b/solution.py
@@ -39,7 +39,7 @@
     lower_factor = jnp.linalg.cholesky(gram_matrix)
     basis_rows = lax.linalg.triangular_solve(lower_factor, left_factor, left_side=True, lower=True)
     right_term = jnp.dot(basis_rows, corrected, precision=highest)
-    right_total = lax.psum(right_term, ("replica", "inner"))
+    right_total = lax.psum(lax.psum(right_term, "replica"), "inner")
     right_factor = right_total / replicas
     embed_step = lax.dot_general(
         basis_rows, right_factor, (((0,), (0,)), ((), ())), precision=highest

time: 1640 us -> 3020 us (1.84)
  waiting for transfers between devices: 641 us -> 1990 us
    psum x1, waiting for transfers between devices: 561 us -> 1800 us  [local(): right_total = lax.psum(lax.psum(right_term, 'replica'), 'inner')]
    psum x1, waiting for transfers between devices: 79.8 us -> 198 us  [local(): square_sum, broad_sum = lax.psum((square_term, broad_term), 'replica')]
where the time goes in v1:
time: 3020 us; the launch traced here: 2990 us
  waiting for transfers between devices  1990 us (66%)
  blocking collectives  961 us (32%)
    psum x1, waiting for transfers between devices, local(): right_total = lax.psum(lax.psum(right_term, 'replica'), 'inner')  1800 us
    psum x1, blocking collectives, local(): gram_matrix = lax.psum(gram_local, 'inner')  927 us
    psum x1, waiting for transfers between devices, local(): square_sum, broad_sum = lax.psum((square_term, broad_term), 'replica')  198 us
  transfers between devices with their start and end apart: 2, of which 2 were waited for; matrix products, arithmetic and copies ran while one was open for 0% of the time, Pallas kernels for 0%

profile of v1, /device:TPU:1, one launch (start us, length us, event | category | flops | bytes accessed | tf_op | source)
XLA Modules:
  0.0 2991.4 jit_solution(8751161365985808712)
XLA Ops:
  7.2 0.0 copy-start
  7.2 0.0 all-reduce.6.cloned.1.call-start
  7.2 1.5 bitcast_add_fusion
  8.7 0.0 copy-done
  8.7 0.7 convolution_bitcast_fusion
  9.4 33.8 %psum.44 = f32[64,128]{1,0:T(8,128)S(1)} all-reduce(f32[64,128]{1,0:T(8,128)S(1)} %convolution_bitcast_fusion), channel_id=1, replica_groups=mesh['replica'=4,'inner'=128] {'replica'}, use_global_device_ids=true, to_apply=%region_2.0 | all-reduce | flops 8192 | bytes 65536 | tf_op jit(solution)/shard_map/psum | solution.py:36
  43.2 0.2 fusion.8
  43.4 926.7 %psum.45 = f32[64,64]{0,1:T(8,128)S(1)} all-reduce(f32[64,64]{0,1:T(8,128)S(1)} %fusion.8), channel_id=1, replica_groups=mesh['replica'=4,'inner'=128] {'inner'}, use_global_device_ids=true, to_apply=%region_3.0 | all-reduce | flops 4096 | bytes 32768 | tf_op jit(solution)/shard_map/psum | solution.py:38
  970.1 0.1 copy.19
  970.2 5.8 cholesky.16
  976.1 0.6 compare_reduce_fusion
  976.7 0.7 fusion.3
  977.4 4.9 custom-call.6
  982.3 0.3 fusion.4
  982.5 0.0 copy-start.2
  982.5 0.0 copy-start.5
  982.6 1.1 fusion.17
  983.7 0.0 copy-done.2
  983.7 0.0 copy-done.5
  983.7 0.0 copy-start.4
  983.7 0.0 copy-start.8
  983.7 0.7 bitcast_subtract_fusion.1
  984.4 0.2 copy-done.4
  984.5 0.1 copy-done.8
  984.6 0.6 bitcast_subtract_fusion.2
  985.3 0.0 copy-start.6
  985.3 0.0 all-reduce.6.cloned.1.call-update
  985.3 0.0 all-reduce.4.cloned.1.call-start
  985.3 198.2 %all-reduce.6.cloned.1.call-done = (f32[2,8,1024]{2,1,0:T(8,128)}, f32[2,8,2048]{2,1,0:T(8,128)}, f32[64,1024]{1,0:T(8,128)}) async-done(((f32[2,8,1024]{2,1,0:T(8,128)}, f32[2,8,2048]{2,1,0:T(8,128)}, f32[64,1024]{1,0:T(8,128)}), (f32[2,8,1024]{2,1,0:T(8,128)}, f32[2,8,2048]{2,1,0:T(8,128)}, f32[64,1024]{1,0:T(8,128)})) %all-reduce.6.cloned.1.call-update) | async-done | bytes 458768 | tf_op jit(solution)/shard_map/psum | solution.py:34
  1183.6 0.0 copy-start.7
  1183.6 0.0 copy-start.9
  1183.6 0.0 copy-start.3
  1183.6 0.0 all-reduce.4.cloned.1.call-update
  1183.6 0.0 copy-start.1
  1183.6 0.0 copy-done.6
  1183.6 0.9 copy-done.7
  1184.5 0.7 multiply_subtract_fusion.1
  1185.2 0.0 copy-done.9
  1185.2 1.5 multiply_subtract_fusion.2
  1186.7 1795.0 %all-reduce.4.cloned.1.call-done = f32[64,1024]{1,0:T(8,128)} async-done(((f32[64,1024]{1,0:T(8,128)}), f32[64,1024]{1,0:T(8,128)}) %all-reduce.4.cloned.1.call-update) | async-done | bytes 262160 | tf_op jit(solution)/shard_map/psum | solution.py:42
  2981.7 0.0 copy-done.3
  2981.8 0.0 copy-done.1
  2981.8 2.8 multiply_subtract_fusion
  (2 shorter events, 0.0 us)
Async XLA Ops:
  7.2 1.6 copy-start
  7.2 1176.4 %all-reduce.6.cloned.1.call-start = ((), (), s32[]{:S(2)}) async-start(), calls=%async_computation.1 | async-start | bytes 917504 | tf_op jit(solution)/shard_map/psum | solution.py:34
  982.5 1.2 copy-start.2
  982.5 1.2 copy-start.5
  983.7 0.8 copy-start.4
  983.7 0.9 copy-start.8
  985.3 198.4 %copy-start.6 = (f32[2,8,2048]{2,1,0:T(8,128)S(1)}, f32[2,8,2048]{2,1,0:T(8,128)}, u32[]{:S(2)}) copy-start(f32[2,8,2048]{2,1,0:T(8,128)} %param.16) | copy-start | bytes 393220
  985.3 1996.5 %all-reduce.4.cloned.1.call-start = ((), (), s32[]{:S(2)}) async-start(), calls=%async_computation | async-start | bytes 524288 | tf_op jit(solution)/shard_map/psum | solution.py:42
  1183.6 0.9 copy-start.7
  1183.6 1.6 copy-start.9
  1183.6 1798.2 %copy-start.3 = (f32[128,1024]{1,0:T(8,128)S(1)}, f32[128,1024]{1,0:T(8,128)}, u32[]{:S(2)}) copy-start(f32[128,1024]{1,0:T(8,128)} %param.19) | copy-start | bytes 1572868
  1183.6 1798.2 %copy-start.1 = (f32[128,1024]{1,0:T(8,128)S(1)}, f32[128,1024]{1,0:T(8,128)}, u32[]{:S(2)}) copy-start(f32[128,1024]{1,0:T(8,128)} %param.17) | copy-start | bytes 1572868
Sparse Core Ops, SparseCore 0:
  985.4 198.1 all-reduce.5
  1186.7 1794.9 all-reduce.3

commit v2 on v0

--- a/solution.py
+++ b/solution.py
@@ -33,7 +33,7 @@
     corrected = embed_weights - embed_copies[0] + embed_error[0]
     square_sum, broad_sum = lax.psum((square_term, broad_term), "replica")
     left_local = lax.dot_general(warm_start, corrected, contract_last, precision=highest)
-    left_factor = lax.psum(left_local, "replica") / replicas
+    left_factor = jnp.sum(lax.all_gather(left_local, "replica"), axis=0) / replicas
     gram_local = lax.dot_general(left_factor, left_factor, contract_last, precision=highest)
     gram_matrix = lax.psum(gram_local, "inner")
     lower_factor = jnp.linalg.cholesky(gram_matrix)

time: 1640 us -> 1620 us (0.988)
    psum x1 -> x0, blocking collectives: 33.8 us -> none  [local(): left_factor = lax.psum(left_local, 'replica') / replicas]
    all_gather x0 -> x1, blocking collectives: none -> 20.8 us  [local(): lax.all_gather(left_local, 'replica')]
where the time goes in v2:
time: 1620 us
  blocking collectives  947 us (58%)
  waiting for transfers between devices  637 us (39%)
  other arithmetic  17.2 us (1%)
    psum x1, blocking collectives, local(): gram_matrix = lax.psum(gram_local, 'inner')  926 us
    psum x1, waiting for transfers between devices, local(): right_total = lax.psum(right_term, ('replica', 'inner'))  557 us
    psum x1, waiting for transfers between devices, local(): square_sum, broad_sum = lax.psum((square_term, broad_term), 'replica')  79.8 us
  transfers between devices with their start and end apart: 2, of which 2 were waited for; matrix products, arithmetic and copies ran while one was open for 0% of the time, Pallas kernels for 0%

profile of v2, /device:TPU:1, one launch (start us, length us, event | category | flops | bytes accessed | tf_op | source)
XLA Modules:
  0.0 1621.0 jit_solution(15205912772731341858)
XLA Ops:
  7.2 0.0 copy-start
  7.2 0.0 all-reduce.4.cloned.1.call-start
  7.2 1.5 bitcast_add_fusion
  8.7 0.0 copy-done
  8.7 0.7 convolution_bitcast_fusion
  9.4 20.8 %all-gather = f32[256,128]{1,0:T(8,128)S(1)} all-gather(f32[64,128]{1,0:T(8,128)S(1)} %convolution_bitcast_fusion), channel_id=2, replica_groups=mesh['replica'=4,'inner'=128] {'replica'}, dimensions={0}, use_global_device_ids=true | all-gather | bytes 163840 | tf_op jit(solution)/shard_map/all_gather | solution.py:36
  30.3 0.2 fusion.8
  30.5 926.2 %psum.30 = f32[64,64]{0,1:T(8,128)S(1)} all-reduce(f32[64,64]{0,1:T(8,128)S(1)} %fusion.8), channel_id=1, replica_groups=mesh['replica'=4,'inner'=128] {'inner'}, use_global_device_ids=true, to_apply=%region_3.0 | all-reduce | flops 4096 | bytes 32768 | tf_op jit(solution)/shard_map/psum | solution.py:38
  956.7 0.1 copy.19
  956.8 5.8 cholesky.16
  962.6 0.6 compare_reduce_fusion
  963.3 0.7 fusion.3
  963.9 4.9 custom-call.6
  968.8 0.3 fusion.4
  969.1 0.0 copy-start.2
  969.1 0.0 copy-start.5
  969.1 0.0 copy-start.4
  969.1 0.0 copy-start.7
  969.1 1.1 fusion.17
  970.3 0.0 copy-start.1
  970.3 0.0 copy-start.3
  970.3 0.0 all-reduce.4.cloned.1.call-update
  970.3 0.0 all-reduce.6.cloned.1.call-start
  970.4 0.0 copy-done.2
  970.4 0.0 copy-done.5
  970.4 0.7 bitcast_subtract_fusion.1
  971.1 0.0 copy-done.4
  971.1 0.0 copy-done.7
  971.1 0.6 bitcast_subtract_fusion.2
  971.7 0.0 all-reduce.6.cloned.1.call-update
  971.7 0.0 copy-start.6
  971.7 557.5 %all-reduce.4.cloned.1.call-done = f32[64,1024]{1,0:T(8,128)} async-done(((f32[64,1024]{1,0:T(8,128)}), f32[64,1024]{1,0:T(8,128)}) %all-reduce.4.cloned.1.call-update) | async-done | bytes 262160 | tf_op jit(solution)/shard_map/psum | solution.py:42
  1529.2 0.0 copy-done.1
  1529.2 0.0 copy-done.3
  1529.2 2.8 multiply_subtract_fusion
  1532.0 79.8 %all-reduce.6.cloned.1.call-done = (f32[2,8,1024]{2,1,0:T(8,128)}, f32[2,8,2048]{2,1,0:T(8,128)}) async-done(((f32[2,8,1024]{2,1,0:T(8,128)}, f32[2,8,2048]{2,1,0:T(8,128)}), (f32[2,8,1024]{2,1,0:T(8,128)}, f32[2,8,2048]{2,1,0:T(8,128)})) %all-reduce.6.cloned.1.call-update) | async-done | bytes 196624 | tf_op jit(solution)/shard_map/psum | solution.py:34
  1611.8 0.0 copy-done.6
  1611.8 0.0 copy-start.8
  1611.8 0.0 copy-start.9
  1611.8 1.7 multiply_subtract_fusion.1
  1613.5 0.0 copy-done.8
  1613.5 0.0 copy-done.9
  1613.5 0.7 multiply_subtract_fusion.2
  (3 shorter events, 0.0 us)
Async XLA Ops:
  7.2 1.6 copy-start
  7.2 1522.0 %all-reduce.4.cloned.1.call-start = ((), (), s32[]{:S(2)}) async-start(), calls=%async_computation | async-start | bytes 524288 | tf_op jit(solution)/shard_map/psum | solution.py:42
  969.1 1.3 copy-start.2
  969.1 1.3 copy-start.5
  969.1 1.9 copy-start.4
  969.1 1.9 copy-start.7
  970.3 558.9 %copy-start.1 = (f32[128,1024]{1,0:T(8,128)S(1)}, f32[128,1024]{1,0:T(8,128)}, u32[]{:S(2)}) copy-start(f32[128,1024]{1,0:T(8,128)} %param.17) | copy-start | bytes 1572868
  970.3 558.9 %copy-start.3 = (f32[128,1024]{1,0:T(8,128)S(1)}, f32[128,1024]{1,0:T(8,128)}, u32[]{:S(2)}) copy-start(f32[128,1024]{1,0:T(8,128)} %param.19) | copy-start | bytes 1572868
  970.3 641.5 %all-reduce.6.cloned.1.call-start = ((), (), s32[]{:S(2)}) async-start(), calls=%async_computation.1 | async-start | bytes 393216 | tf_op jit(solution)/shard_map/psum | solution.py:34
  971.7 640.1 %copy-start.6 = (f32[2,8,2048]{2,1,0:T(8,128)S(1)}, f32[2,8,2048]{2,1,0:T(8,128)}, u32[]{:S(2)}) copy-start(f32[2,8,2048]{2,1,0:T(8,128)} %param.16) | copy-start | bytes 393220
  1611.8 1.7 copy-start.8
  1611.8 1.7 copy-start.9
Sparse Core Ops, SparseCore 0:
  970.4 558.7 all-reduce.3
  1533.0 78.7 all-reduce.5
